TPU v7x, 512 devices: a whole 4x8x8 slice. The times are simulated.
512 devices in a mesh: batch: 32 (over y_lo, z), seq: 16 (over y_hi, x, core).
Axes of the slice: x: 4, y: 8 (y_hi: 2, y_lo: 4; y = y_hi * 4 + y_lo), z: 8, core: 2. Of those that a mesh axis runs over, the one named last changes fastest.
Arguments:
- sequence_input: bfloat16 [32, 4096, 768], P('batch', 'seq'), may hold values from -64 to 64
- bn_gain: float32 [768], replicated, may hold values from 0.1 to 1.9
- bn_bias: float32 [768], replicated, may hold values from -3 to 3
- conv_weight: bfloat16 [5, 768, 768], P(None, None, 'batch'), may hold values from -0.09375 to 0.09375
- conv_bias: float32 [768], replicated, may hold values from -3 to 3
- ln_gain: float32 [768], replicated, may hold values from 0.1 to 1.9
- ln_bias: float32 [768], replicated, may hold values from -3 to 3
- qkv_weight: bfloat16 [768, 1792], P(None, 'batch'), may hold values from -32 to 32
Outputs:
- pooled: bfloat16 [32, 2048, 768], P('batch', 'seq')
- attended: bfloat16 [32, 2048, 768], P('batch', 'seq')
All inputs are finite; a program needn't handle non-finite values.
Results may differ from a plain program's by a relative error of at most 0.025.
The roundings to bfloat16 on the way count: a program that leaves them out, or rounds other values in their place, can miss the bound.
Values may be sent and summed in bfloat16 or wider, within the bound.
No kernel may reach another device: no remote copies, remote signals or barrier semaphores. Data moves between devices by JAX's collectives and lax.ppermute only.
A program may use at most 64 MiB of HBM per device.

v0:
```python
import jax
import jax.numpy as jnp
from jax import lax
from jax.sharding import PartitionSpec as P

HEADS = 8
KEY = 64
VAL = 96
epsilon = 1e-05


def extended(cells, sides, width):
    for axis, dim in sides:
        count = lax.axis_size(axis)
        ends = count - 1
        head = lax.slice_in_dim(cells, 0, width, axis=dim)
        tail = lax.slice_in_dim(cells, cells.shape[dim] - width, cells.shape[dim], axis=dim)
        cells = jnp.concatenate(
            [
                lax.ppermute(tail, axis, [(i, (i + 1) % count) for i in range(ends)]),
                cells,
                lax.ppermute(head, axis, [((i + 1) % count, i) for i in range(ends)]),
            ],
            axis=dim,
        )
    return cells


def conv_taps(padded, kernel, positions):
    result = None
    for tap_index in range(kernel.shape[0]):
        window = padded[:, tap_index : tap_index + positions]
        product = jnp.einsum(
            "slc,co->slo", window, kernel[tap_index], preferred_element_type=jnp.float32
        )
        result = product if result is None else result + product
    return result


def online_step(carry, query_rows, key_block, value_block):
    best, weight_sum, accum = carry
    scores = jnp.einsum(
        "sqhk,sjhk->shqj", query_rows, key_block, preferred_element_type=jnp.float32
    )
    newest = jnp.maximum(best, jnp.max(scores, axis=-1))
    fade = jnp.exp(best - newest)
    weights = jnp.exp(scores - newest[..., None])
    weight_sum = weight_sum * fade + jnp.sum(weights, axis=-1)
    accum = accum * fade[..., None] + jnp.einsum(
        "shqj,sjhv->shqv",
        weights.astype(jnp.bfloat16),
        value_block,
        preferred_element_type=jnp.float32,
    )
    return (newest, weight_sum, accum)


def blocked_attend(carry, query_rows, key_piece, value_piece):
    rows = key_piece.shape[1]
    block = min(rows, 512)
    for first in range(0, rows, block):
        carry = online_step(
            carry,
            query_rows,
            key_piece[:, first : first + block],
            value_piece[:, first : first + block],
        )
    return carry


def empty_state(seqs_here, heads_here, rows):
    return (
        jnp.full((seqs_here, heads_here, rows), -jnp.inf, jnp.float32),
        jnp.zeros((seqs_here, heads_here, rows), jnp.float32),
        jnp.zeros((seqs_here, heads_here, rows, VAL), jnp.float32),
    )


def on_device(
    sequence_input, bn_gain, bn_bias, conv_weight, conv_bias, ln_gain, ln_bias, qkv_weight
):
    seqs_here = sequence_input.shape[0]
    positions = sequence_input.shape[1]
    channels = sequence_input.shape[2]
    values_in = sequence_input.astype(jnp.float32)
    total, squares = lax.psum(
        (jnp.sum(values_in, axis=(0, 1)), jnp.sum(values_in * values_in, axis=(0, 1))),
        ("batch", "seq"),
    )
    count = float(seqs_here * positions * lax.axis_size("batch") * lax.axis_size("seq"))
    mean = total / count
    var = squares / count - mean * mean
    activated = jax.nn.gelu(
        (values_in - mean) * lax.rsqrt(var + epsilon) * bn_gain + bn_bias, approximate=True
    ).astype(jnp.bfloat16)
    padded = extended(activated, (("seq", 1),), 2)
    conv_out = conv_taps(
        padded, lax.all_gather(conv_weight, "batch", axis=2, tiled=True), positions
    )
    conv_out = conv_out + conv_bias
    bins_here = positions // 2
    pooled = conv_out.reshape(seqs_here, bins_here, 2, channels).max(axis=2).astype(jnp.bfloat16)
    pooled_wide = pooled.astype(jnp.float32)
    centre = jnp.mean(pooled_wide, axis=-1, keepdims=True)
    spread = jnp.mean((pooled_wide - centre) ** 2, axis=-1, keepdims=True)
    normed = ((pooled_wide - centre) * lax.rsqrt(spread + epsilon) * ln_gain + ln_bias).astype(
        jnp.bfloat16
    )
    proj = jnp.einsum(
        "sbd,dk->sbk",
        normed,
        lax.all_gather(qkv_weight, "batch", axis=1, tiled=True),
        preferred_element_type=jnp.float32,
    )
    head_keys = HEADS * KEY
    queries = (proj[..., :head_keys] * KEY ** (-0.5)).astype(jnp.bfloat16)
    key_rows = proj[..., head_keys : 2 * head_keys].astype(jnp.bfloat16)
    value_rows = proj[..., 2 * head_keys :].astype(jnp.bfloat16)
    query_heads = queries.reshape(seqs_here, bins_here, HEADS, KEY)
    key_piece = lax.all_gather(key_rows, "seq", axis=1, tiled=True)
    value_piece = lax.all_gather(value_rows, "seq", axis=1, tiled=True)
    width_now = key_piece.shape[1]
    best, weight_sum, accum = blocked_attend(
        empty_state(seqs_here, HEADS, bins_here),
        query_heads,
        key_piece.reshape(seqs_here, width_now, HEADS, KEY),
        value_piece.reshape(seqs_here, width_now, HEADS, VAL),
    )
    attended = (
        (accum / weight_sum[..., None])
        .transpose(0, 2, 1, 3)
        .reshape(seqs_here, bins_here, HEADS * VAL)
        .astype(jnp.bfloat16)
    )
    return (pooled, attended)


def solution(mesh):
    placed = (
        P("batch", "seq", None),
        P(),
        P(),
        P(None, None, "batch"),
        P(),
        P(),
        P(),
        P(None, "batch"),
    )
    return jax.shard_map(
        on_device,
        mesh=mesh,
        in_specs=placed,
        out_specs=(P("batch", "seq", None), P("batch", "seq", None)),
        check_vma=False,
    )
```

profile of v0, /device:TPU:1, one launch (start us, length us, event | category | flops | bytes accessed | tf_op | source)
XLA Modules:
  0.0 494.9 jit_solution(5999719984073595939)
XLA Ops:
  7.2 0.0 all-gather.5.cloned.1.call-start
  7.2 0.7 all-gather.5.cloned.1.call-update
  7.9 0.0 all-gather.7.cloned.1.call-start
  7.9 0.7 all-gather.7.cloned.1.call-update
  8.6 0.0 all-gather.9.cloned.1.call-start
  8.7 1.1 convert_reduce_fusion
  9.8 109.2 %all-reduce = (f32[768]{0:T(1024)S(1)}, f32[768]{0:T(1024)S(1)}) all-reduce(f32[768]{0:T(1024)S(1)} %get-tuple-element.7, f32[768]{0:T(1024)S(1)} %get-tuple-element.6), channel_id=1, replica_groups=mesh['batch'=32,'seq'=16] {'batch','seq'}, use_global_device_ids=true, to_apply=%region_3.0 | all-reduce | flops 1536 | bytes 12288 | tf_op jit(solution)/shard_map/psum | solution.py:86
  119.0 1.4 fusion.28
  120.5 5.3 %collective-permute-start = (bf16[1,2,768]{2,1,0:T(2,128)(2,1)S(1)}, bf16[1,2,768]{2,1,0:T(2,128)(2,1)S(1)}, u32[]{:S(2)}, u32[]{:S(2)}) collective-permute-start(bf16[1,2,768]{2,1,0:T(2,128)(2,1)S(1)} %get-tuple-element.18), channel_id=1, source_target_pairs={{0,1},{1,2},{2,3},{3,4},{4,5},{5,6},{6,7},{7,8},{8,9},{9,10},{10,1... | collective-permute-start | bytes 9224 | tf_op jit(solution)/shard_map/ppermute | solution.py:20
  125.8 1.9 collective-permute-start.1
  127.7 0.0 collective-permute-done
  127.7 33.8 %all-gather.5.cloned.1.call-done = bf16[5,768,768]{1,2,0:T(8,128)(2,1)} async-done(((bf16[5,768,24]{1,2,0:T(8,128)(2,1)}), bf16[5,768,768]{1,2,0:T(8,128)(2,1)}) %all-gather.5.cloned.1.call-update) | async-done | bytes 5898256 | tf_op jit(solution)/shard_map/all_gather | solution.py:98
  161.5 1.9 fusion.13
  163.4 1.9 convolution_add_fusion.3
  165.4 0.0 copy-done.9
  165.4 0.5 convolution_add_fusion.2
  165.9 0.0 copy-start.12
  165.9 0.0 collective-permute-done.1
  165.9 0.5 convolution_add_fusion.1
  166.4 0.1 copy-done.12
  166.6 0.5 fusion.8
  167.1 0.1 reshape.416
  167.3 1.0 reduce_max.45
  168.3 0.0 copy-start.8
  168.3 0.1 convert_reduce_fusion.1
  168.4 0.2 multiply_reduce_fusion
  168.6 146.7 %all-gather.7.cloned.1.call-done = bf16[768,1792]{0,1:T(8,128)(2,1)} async-done(((bf16[768,56]{0,1:T(8,128)(2,1)}), bf16[768,1792]{0,1:T(8,128)(2,1)}) %all-gather.7.cloned.1.call-update) | async-done | bytes 2752528 | tf_op jit(solution)/shard_map/all_gather | solution.py:112
  315.3 0.0 copy-done.10
  315.3 0.0 copy-done.11
  315.3 2.8 fusion.69
  318.1 0.0 copy-done.8
  318.2 0.6 slice.106
  318.8 0.0 all-gather.9.cloned.1.call-update
  318.8 0.2 all-gather.11.cloned.1.call-start
  319.1 0.7 slice.108
  319.7 0.0 all-gather.11.cloned.1.call-update
  319.8 0.1 copy.23
  319.9 81.3 %all-gather.9.cloned.1.call-done = bf16[1,2048,512]{2,1,0:T(8,128)(2,1)} async-done(((bf16[1,128,512]{2,1,0:T(8,128)(2,1)}), bf16[1,2048,512]{2,1,0:T(8,128)(2,1)}) %all-gather.9.cloned.1.call-update) | async-done | bytes 2097168 | tf_op jit(solution)/shard_map/all_gather | solution.py:120
  401.3 2.9 copy.24
  404.2 0.0 copy-start.6
  404.2 1.4 copy-done.6
  405.6 0.6 fusion.71
  406.1 0.0 copy-start.7
  406.1 2.2 fusion.72
  408.3 0.3 copy-done.7
  408.6 0.6 fusion.73
  409.2 0.6 fusion.70
  409.8 0.0 copy-done.4
  409.8 1.2 fusion
  411.0 0.2 copy-done.2
  411.2 0.0 copy-done
  411.2 1.2 fusion.2
  412.4 63.9 %all-gather.11.cloned.1.call-done = bf16[1,2048,768]{2,1,0:T(8,128)(2,1)} async-done(((bf16[1,128,768]{2,1,0:T(8,128)(2,1)}), bf16[1,2048,768]{2,1,0:T(8,128)(2,1)}) %all-gather.11.cloned.1.call-update) | async-done | bytes 3145744 | tf_op jit(solution)/shard_map/all_gather | solution.py:121
  476.3 4.7 copy.25
  481.0 2.5 fusion.12
  483.4 0.0 copy-start.3
  483.4 0.0 copy-done.1
  483.5 1.8 fusion.11
  485.3 0.0 copy-start.5
  485.3 0.3 copy-done.3
  485.6 0.6 fusion.10
  486.2 0.8 copy-done.5
  487.0 0.6 fusion.14
  487.6 0.8 copy.26
  (14 shorter events, 0.1 us)
Async XLA Ops:
  7.2 154.3 %all-gather.5.cloned.1.call-start = ((), (), s32[]{:S(2)}) async-start(), calls=%async_computation | async-start | bytes 6082560 | tf_op jit(solution)/shard_map/all_gather | solution.py:98
  7.9 307.4 %all-gather.7.cloned.1.call-start = ((), (), s32[]{:S(2)}) async-start(), calls=%async_computation.1 | async-start | bytes 2838528 | tf_op jit(solution)/shard_map/all_gather | solution.py:112
  8.6 392.6 %all-gather.9.cloned.1.call-start = ((), (), s32[]{:S(2)}) async-start(), calls=%async_computation.2 | async-start | bytes 2228224 | tf_op jit(solution)/shard_map/all_gather | solution.py:120
  120.5 7.3 %collective-permute-start = (bf16[1,2,768]{2,1,0:T(2,128)(2,1)S(1)}, bf16[1,2,768]{2,1,0:T(2,128)(2,1)S(1)}, u32[]{:S(2)}, u32[]{:S(2)}) collective-permute-start(bf16[1,2,768]{2,1,0:T(2,128)(2,1)S(1)} %get-tuple-element.18), channel_id=1, source_target_pairs={{0,1},{1,2},{2,3},{3,4},{4,5},{5,6},{6,7},{7,8},{8,9},{9,10},{10,1... | collective-permute-start | bytes 9224 | tf_op jit(solution)/shard_map/ppermute | solution.py:20
  125.8 40.1 %collective-permute-start.1 = (bf16[1,2,768]{2,1,0:T(2,128)(2,1)S(1)}, bf16[1,2,768]{2,1,0:T(2,128)(2,1)S(1)}, u32[]{:S(2)}, u32[]{:S(2)}) collective-permute-start(bf16[1,2,768]{2,1,0:T(2,128)(2,1)S(1)} %get-tuple-element.17), channel_id=1, source_target_pairs={{1,0},{2,1},{3,2},{4,3},{5,4},{6,5},{7,6},{8,7},{9,8},{10,9},{11,1... | collective-permute-start | bytes 9224 | tf_op jit(solution)/shard_map/ppermute | solution.py:22
  161.5 3.9 copy-start.9
  165.9 0.7 copy-start.12
  166.6 148.7 %copy-start.10 = (f32[768]{0:T(1024)S(1)}, f32[768]{0:T(1024)}, u32[]{:S(2)}) copy-start(f32[768]{0:T(1024)} %param.14) | copy-start | bytes 9220
  166.6 148.7 %copy-start.11 = (f32[768]{0:T(1024)S(1)}, f32[768]{0:T(1024)}, u32[]{:S(2)}) copy-start(f32[768]{0:T(1024)} %param.13) | copy-start | bytes 9220
  168.3 149.8 %copy-start.8 = (bf16[128,768]{1,0:T(8,128)(2,1)}, bf16[128,768]{1,0:T(8,128)(2,1)S(1)}, u32[]{:S(2)}) copy-start(bf16[128,768]{1,0:T(8,128)(2,1)S(1)} %reduce_max.45) | copy-start | bytes 589828
  318.8 157.4 %all-gather.11.cloned.1.call-start = ((), (), s32[]{:S(2)}) async-start(), calls=%async_computation.3 | async-start | bytes 3342336 | tf_op jit(solution)/shard_map/all_gather | solution.py:121
  404.2 1.4 copy-start.6
  406.1 3.7 copy-start.4
  406.1 2.5 copy-start.7
  409.2 2.0 copy-start
  409.8 1.4 copy-start.2
  481.0 2.5 copy-start.1
  483.4 2.1 copy-start.3
  485.3 1.7 copy-start.5
Sparse Core Ops, SparseCore 0:
  10.1 151.3 all-gather.4
  163.6 151.6 all-gather.6
  318.9 82.2 all-gather.8
  405.0 71.1 all-gather.10
where the time goes:
time: 495 us
  waiting for transfers between devices  327 us (66%)
  blocking collectives  109 us (22%)
  matrix products  17.5 us (4%)
  between operations  14 us (3%)
  local copies, waits for them, and re-layouts  13.2 us (3%)
  starting transfers between devices  7.58 us (2%)
  other arithmetic  6.26 us (1%)
    all_gather x1, waiting for transfers between devices, on_device(): lax.all_gather(qkv_weight, 'batch', axis=1, tiled=True)  147 us
    psum x1, blocking collectives, on_device(): lax.psum((jnp.sum(values_in, axis=(0, 1)), jnp.sum(values_in * values_in,...  109 us
    all_gather x1, waiting for transfers between devices, on_device(): key_piece = lax.all_gather(key_rows, 'seq', axis=1, tiled=True)  81.3 us
    all_gather x1, waiting for transfers between devices, on_device(): value_piece = lax.all_gather(value_rows, 'seq', axis=1, tiled=True)  63.9 us
    all_gather x1, waiting for transfers between devices, on_device(): lax.all_gather(conv_weight, 'batch', axis=2, tiled=True)  33.8 us
  transfers between devices with their start and end apart: 6, of which 4 were waited for; matrix products, arithmetic and copies ran while one was open for 4% of the time, Pallas kernels for 0%

commit v1 on v0

--- a/solution.py
+++ b/solution.py
@@ -1,3 +1,4 @@
+import functools
 import jax
 import jax.numpy as jnp
 from jax import lax
@@ -7,6 +8,15 @@
 KEY = 64
 VAL = 96
 epsilon = 1e-05
+
+
+def mark_strings_on(my_tile, axis_tag):
+    local_part = jnp.stack([my_tile for _ in range(lax.axis_size(axis_tag))])
+    now = lax.all_to_all(local_part, axis_name=axis_tag, concat_axis=0, split_axis=0)
+    return jnp.concatenate(now, axis=1)
+
+
+connect_the_ladders = functools.partial(mark_strings_on, axis_tag="seq")
 
 
 def extended(cells, sides, width):
@@ -118,7 +128,7 @@
     value_rows = proj[..., 2 * head_keys :].astype(jnp.bfloat16)
     query_heads = queries.reshape(seqs_here, bins_here, HEADS, KEY)
     key_piece = lax.all_gather(key_rows, "seq", axis=1, tiled=True)
-    value_piece = lax.all_gather(value_rows, "seq", axis=1, tiled=True)
+    value_piece = connect_the_ladders(value_rows)
     width_now = key_piece.shape[1]
     best, weight_sum, accum = blocked_attend(
         empty_state(seqs_here, HEADS, bins_here),

time: 495 us -> 477 us (0.964)
  the two profiles are of different devices: /device:TPU:1 before, /device:TPU:25 now
where the time goes in v1:
time: 477 us; the launch traced here: 476 us
  waiting for transfers between devices  272 us (57%)
  blocking collectives  109 us (23%)
  starting transfers between devices  35.5 us (7%)
  local copies, waits for them, and re-layouts  20.7 us (4%)
  matrix products  18.5 us (4%)
  between operations  14 us (3%)
  other arithmetic  6.27 us (1%)
    all_gather x1, waiting for transfers between devices, on_device(): lax.all_gather(qkv_weight, 'batch', axis=1, tiled=True)  147 us
    psum x1, blocking collectives, on_device(): lax.psum((jnp.sum(values_in, axis=(0, 1)), jnp.sum(values_in * values_in,...  109 us
    all_gather x1, waiting for transfers between devices, on_device(): key_piece = lax.all_gather(key_rows, 'seq', axis=1, tiled=True)  101 us
    all_to_all x1, starting transfers between devices, mark_strings_on(): lax.all_to_all(local_part, axis_name=axis_tag, concat_axis=0, split_axis=0)  28.3 us
    all_gather x1, waiting for transfers between devices, on_device(): lax.all_gather(conv_weight, 'batch', axis=2, tiled=True)  23.5 us
  transfers between devices with their start and end apart: 6, of which 3 were waited for; matrix products, arithmetic and copies ran while one was open for 5% of the time, Pallas kernels for 0%

profile of v1, /device:TPU:25, one launch (start us, length us, event | category | flops | bytes accessed | tf_op | source)
XLA Modules:
  0.0 476.4 jit_solution(3661006029860878029)
XLA Ops:
  7.2 0.0 all-gather.4.cloned.1.call-start
  7.2 0.7 all-gather.4.cloned.1.call-update
  7.9 0.0 all-gather.6.cloned.1.call-start
  7.9 0.7 all-gather.6.cloned.1.call-update
  8.6 0.0 all-gather.8.cloned.1.call-start
  8.7 1.1 convert_reduce_fusion
  9.8 109.0 %all-reduce = (f32[768]{0:T(1024)S(1)}, f32[768]{0:T(1024)S(1)}) all-reduce(f32[768]{0:T(1024)S(1)} %get-tuple-element.9, f32[768]{0:T(1024)S(1)} %get-tuple-element.8), channel_id=1, replica_groups=mesh['batch'=32,'seq'=16] {'batch','seq'}, use_global_device_ids=true, to_apply=%region_3.0 | all-reduce | flops 1536 | bytes 12288 | tf_op jit(solution)/shard_map/psum | solution.py:96
  118.8 1.4 fusion.28
  120.2 5.2 %collective-permute-start = (bf16[1,2,768]{2,1,0:T(2,128)(2,1)S(1)}, bf16[1,2,768]{2,1,0:T(2,128)(2,1)S(1)}, u32[]{:S(2)}, u32[]{:S(2)}) collective-permute-start(bf16[1,2,768]{2,1,0:T(2,128)(2,1)S(1)} %get-tuple-element.20), channel_id=1, source_target_pairs={{0,1},{1,2},{2,3},{3,4},{4,5},{5,6},{6,7},{7,8},{8,9},{9,10},{10,1... | collective-permute-start | bytes 9224 | tf_op jit(solution)/shard_map/ppermute | solution.py:30
  125.4 1.9 collective-permute-start.1
  127.3 0.0 collective-permute-done
  127.4 23.5 %all-gather.4.cloned.1.call-done = bf16[5,768,768]{1,2,0:T(8,128)(2,1)} async-done(((bf16[5,768,24]{1,2,0:T(8,128)(2,1)}), bf16[5,768,768]{1,2,0:T(8,128)(2,1)}) %all-gather.4.cloned.1.call-update) | async-done | bytes 5898256 | tf_op jit(solution)/shard_map/all_gather | solution.py:108
  150.8 0.0 copy-start.8
  150.8 1.9 fusion.13
  152.8 1.9 convolution_add_fusion.3
  154.7 0.0 copy-done.8
  154.7 0.5 convolution_add_fusion.2
  155.2 0.0 copy-start.11
  155.2 0.0 collective-permute-done.1
  155.2 0.5 convolution_add_fusion.1
  155.8 0.1 copy-done.11
  155.9 0.0 copy-start.9
  155.9 0.5 fusion.8
  156.4 0.1 reshape.416
  156.6 1.0 reduce_max.45
  157.6 0.0 copy-start.7
  157.6 0.1 convert_reduce_fusion.1
  157.8 0.2 multiply_reduce_fusion
  158.0 147.0 %all-gather.6.cloned.1.call-done = bf16[768,1792]{0,1:T(8,128)(2,1)} async-done(((bf16[768,56]{0,1:T(8,128)(2,1)}), bf16[768,1792]{0,1:T(8,128)(2,1)}) %all-gather.6.cloned.1.call-update) | async-done | bytes 2752528 | tf_op jit(solution)/shard_map/all_gather | solution.py:122
  305.0 0.0 copy-done.9
  305.0 0.0 copy-done.10
  305.0 2.8 fusion.69
  307.9 0.0 copy-done.7
  307.9 0.7 slice.106
  308.5 0.0 all-gather.8.cloned.1.call-update
  308.6 0.2 copy.26
  308.7 2.3 stack.2
  311.1 28.3 %all-to-all-start = ((bf16[16,1,128,768]{2,3,1,0:T(8,128)(2,1)}), bf16[16,1,128,768]{2,3,1,0:T(8,128)(2,1)}, u32[]{:S(2)}, u32[]{:S(2)}) async-start(bf16[16,1,128,768]{2,3,1,0:T(8,128)(2,1)} %stack.2), calls=%async_computation | async-start | bytes 6291456 | tf_op jit(solution)/shard_map/all_to_all | solution.py:15
  339.4 0.1 copy.24
  339.5 100.6 %all-gather.8.cloned.1.call-done = bf16[1,2048,512]{2,1,0:T(8,128)(2,1)} async-done(((bf16[1,128,512]{2,1,0:T(8,128)(2,1)}), bf16[1,2048,512]{2,1,0:T(8,128)(2,1)}) %all-gather.8.cloned.1.call-update) | async-done | bytes 2097168 | tf_op jit(solution)/shard_map/all_gather | solution.py:130
  440.1 2.9 copy.25
  443.0 0.0 copy-start.6
  443.0 0.6 fusion.70
  443.6 0.7 copy-done.6
  444.3 0.6 fusion.71
  444.9 2.0 fusion.72
  446.9 1.6 fusion.73
  448.5 0.0 copy-done
  448.5 0.0 copy-done.4
  448.6 1.2 fusion
  449.7 0.1 copy-done.1
  449.8 1.2 fusion.2
  451.0 0.0 all-to-all-done
  451.0 5.6 %copy.27 = bf16[16,1,128,768]{2,0,3,1:T(8,128)(2,1)} copy(bf16[16,1,128,768]{2,3,1,0:T(8,128)(2,1)} %all-to-all-done) | data formatting | bytes 6291456 | tf_op jit(solution)/shard_map/all_to_all | solution.py:15
  456.6 5.8 %reshape_reshape.3 = bf16[1,2048,8,96]{1,3,2,0:T(8,128)(2,1)} reshape(bf16[16,1,128,768]{2,0,3,1:T(8,128)(2,1)} %copy.27) | data formatting | bytes 6291456 | tf_op jit(solution)/shard_map/reshape;reshape | solution.py:137
  462.4 2.5 fusion.12
  464.9 0.0 copy-start.3
  464.9 0.0 copy-done.2
  464.9 1.8 fusion.11
  466.8 0.3 copy-done.3
  467.1 0.6 fusion.10
  467.7 0.8 copy-done.5
  468.4 0.6 fusion.14
  469.0 0.8 copy.28
  (14 shorter events, 0.1 us)
Async XLA Ops:
  7.2 143.7 %all-gather.4.cloned.1.call-start = ((), (), s32[]{:S(2)}) async-start(), calls=%async_computation.1 | async-start | bytes 6082560 | tf_op jit(solution)/shard_map/all_gather | solution.py:108
  7.9 297.1 %all-gather.6.cloned.1.call-start = ((), (), s32[]{:S(2)}) async-start(), calls=%async_computation.2 | async-start | bytes 2838528 | tf_op jit(solution)/shard_map/all_gather | solution.py:122
  8.6 431.4 %all-gather.8.cloned.1.call-start = ((), (), s32[]{:S(2)}) async-start(), calls=%async_computation.3 | async-start | bytes 2228224 | tf_op jit(solution)/shard_map/all_gather | solution.py:130
  120.2 7.1 %collective-permute-start = (bf16[1,2,768]{2,1,0:T(2,128)(2,1)S(1)}, bf16[1,2,768]{2,1,0:T(2,128)(2,1)S(1)}, u32[]{:S(2)}, u32[]{:S(2)}) collective-permute-start(bf16[1,2,768]{2,1,0:T(2,128)(2,1)S(1)} %get-tuple-element.20), channel_id=1, source_target_pairs={{0,1},{1,2},{2,3},{3,4},{4,5},{5,6},{6,7},{7,8},{8,9},{9,10},{10,1... | collective-permute-start | bytes 9224 | tf_op jit(solution)/shard_map/ppermute | solution.py:30
  125.4 29.8 %collective-permute-start.1 = (bf16[1,2,768]{2,1,0:T(2,128)(2,1)S(1)}, bf16[1,2,768]{2,1,0:T(2,128)(2,1)S(1)}, u32[]{:S(2)}, u32[]{:S(2)}) collective-permute-start(bf16[1,2,768]{2,1,0:T(2,128)(2,1)S(1)} %get-tuple-element.19), channel_id=1, source_target_pairs={{1,0},{2,1},{3,2},{4,3},{5,4},{6,5},{7,6},{8,7},{9,8},{10,9},{11,1... | collective-permute-start | bytes 9224 | tf_op jit(solution)/shard_map/ppermute | solution.py:32
  150.8 3.9 copy-start.8
  155.2 0.7 copy-start.11
  155.9 149.1 %copy-start.9 = (f32[768]{0:T(1024)S(1)}, f32[768]{0:T(1024)}, u32[]{:S(2)}) copy-start(f32[768]{0:T(1024)} %param.14) | copy-start | bytes 9220
  155.9 149.1 %copy-start.10 = (f32[768]{0:T(1024)S(1)}, f32[768]{0:T(1024)}, u32[]{:S(2)}) copy-start(f32[768]{0:T(1024)} %param.13) | copy-start | bytes 9220
  157.6 150.2 %copy-start.7 = (bf16[128,768]{1,0:T(8,128)(2,1)}, bf16[128,768]{1,0:T(8,128)(2,1)S(1)}, u32[]{:S(2)}) copy-start(bf16[128,768]{1,0:T(8,128)(2,1)S(1)} %reduce_max.45) | copy-start | bytes 589828
  311.1 139.9 %all-to-all-start = ((bf16[16,1,128,768]{2,3,1,0:T(8,128)(2,1)}), bf16[16,1,128,768]{2,3,1,0:T(8,128)(2,1)}, u32[]{:S(2)}, u32[]{:S(2)}) async-start(bf16[16,1,128,768]{2,3,1,0:T(8,128)(2,1)} %stack.2), calls=%async_computation | async-start | bytes 6291456 | tf_op jit(solution)/shard_map/all_to_all | solution.py:15
  443.0 1.3 copy-start.6
  444.3 4.2 copy-start
  444.9 3.7 copy-start.4
  448.5 1.3 copy-start.1
  462.4 2.5 copy-start.2
  464.9 2.1 copy-start.3
  466.8 1.7 copy-start.5
Sparse Core Ops, SparseCore 0:
  10.1 140.6 all-gather.3
  152.9 152.0 all-gather.5
  308.9 131.1 all-gather.7
